TPU v7x, 32 devices: a whole 2x2x4 slice. The times are simulated.
32 devices in a mesh: fsdp: 4 (over y, x), heads: 2 (over core), tensor: 4 (over z).
Axes of the slice: x: 2, y: 2, z: 4, core: 2. Of those that a mesh axis runs over, the one named last changes fastest.
Arguments:
- inputs: float32 [32, 729, 1152], P(('fsdp', 'heads', 'tensor')), may hold values from -6 to 6
- cotangent: float32 [32, 729, 1152], P(('fsdp', 'heads', 'tensor')), may hold values from -6 to 6
- image_adapter_index: int32 [32], replicated, may hold values from 0 to 7
- first_norm_gain: float32 [1152], replicated, may hold values from 0.5 to 1.5
- first_norm_bias: float32 [1152], replicated, may hold values from -3 to 3
- second_norm_gain: float32 [1152], replicated, may hold values from 0.5 to 1.5
- second_norm_bias: float32 [1152], replicated, may hold values from -3 to 3
- query_key_value_weight: bfloat16 [1152, 3, 1152], P('fsdp', None, 'heads'), may hold values from -0.1875 to 0.1875
- attention_output_weight: bfloat16 [1152, 1152], P('fsdp', 'heads'), may hold values from -3 to 3
- up_weight: bfloat16 [1152, 4304], P('fsdp', 'tensor'), may hold values from -0.1875 to 0.1875
- down_weight: bfloat16 [1152, 4304], P('fsdp', 'tensor'), may hold values from -0.09375 to 0.09375
- up_projection_bias: bfloat16 [4304], P('tensor'), may hold values from -3 to 3
- down_projection_bias: bfloat16 [1152], replicated, may hold values from -3 to 3
- query_key_value_adapter_first: bfloat16 [3, 8, 1152, 16], replicated, may hold values from -0.1875 to 0.1875
- query_key_value_adapter_second: bfloat16 [3, 8, 16, 1152], P(None, None, None, 'heads'), may hold values from -0.75 to 0.75
- projection_adapter_first: bfloat16 [8, 1152, 16], P(None, 'heads'), may hold values from -3 to 3
- projection_adapter_second: bfloat16 [8, 16, 1152], replicated, may hold values from -0.75 to 0.75
- up_adapter_first: bfloat16 [8, 1152, 16], replicated, may hold values from -0.1875 to 0.1875
- up_adapter_second: bfloat16 [8, 16, 4304], P(None, None, 'tensor'), may hold values from -0.75 to 0.75
- down_adapter_first: bfloat16 [8, 16, 4304], P(None, None, 'tensor'), may hold values from -0.09375 to 0.09375
- down_adapter_second: bfloat16 [8, 16, 1152], replicated, may hold values from -0.75 to 0.75
Outputs:
- layer_output: float32 [32, 729, 1152], P(('fsdp', 'heads', 'tensor'))
- grad_input: float32 [32, 729, 1152], P(('fsdp', 'heads', 'tensor'))
- grad_qkv_in: float32 [3, 8, 1152, 16], replicated
- grad_qkv_out: float32 [3, 8, 16, 1152], P(None, None, None, 'heads')
- grad_proj_in: float32 [8, 1152, 16], P(None, 'heads')
- grad_proj_out: float32 [8, 16, 1152], replicated
- grad_up_in: float32 [8, 1152, 16], replicated
- grad_up_out: float32 [8, 16, 4304], P(None, None, 'tensor')
- grad_down_in: float32 [8, 16, 4304], P(None, None, 'tensor')
- grad_down_out: float32 [8, 16, 1152], replicated
All inputs are finite; a program needn't handle non-finite values.
Results may differ from a plain program's by a relative error of at most 0.02.
Values may be sent and summed in bfloat16 or wider, within the bound.
A program may use at most 256 MiB of HBM per device.

v0:
```python
import jax
import jax.numpy as jnp
from jax import lax
from jax.sharding import PartitionSpec as P

HEAD_DIM = 72
highest_precision = lax.Precision.HIGHEST
norm_eps = 1e-06


def normalize(values, gain, bias):
    mean = jnp.mean(values, axis=-1, keepdims=True)
    centred = values - mean
    inverse = lax.rsqrt(jnp.mean(centred * centred, axis=-1, keepdims=True) + norm_eps)
    unit = centred * inverse
    return (unit * gain + bias, unit, inverse)


def normalize_back(grad_norm, unit, inverse, gain):
    scaled = grad_norm * gain
    return inverse * (
        scaled
        - jnp.mean(scaled, axis=-1, keepdims=True)
        - unit * jnp.mean(scaled * unit, axis=-1, keepdims=True)
    )


def gelu_tanh(values):
    return jax.nn.gelu(values, approximate=True)


def one_hot(ids, count):
    return (ids[:, None] == jnp.arange(count, dtype=jnp.int32)[None, :]).astype(jnp.float32)


def by_adapter(hot, per_image):
    return jnp.einsum("ia,ixy->axy", hot, per_image, precision=highest_precision)


def attend_forward(operands):
    query, keyed, valued = operands
    scores = jnp.einsum(
        "qhd,khd->hqk", query, keyed, preferred_element_type=jnp.float32
    ) * HEAD_DIM ** (-0.5)
    top = jnp.max(scores, axis=-1, keepdims=True)
    weights = jnp.exp(scores - top)
    total = jnp.sum(weights, axis=-1, keepdims=True)
    probs = (weights / total).astype(jnp.bfloat16)
    mixed_heads = jnp.einsum("hqk,khd->qhd", probs, valued, preferred_element_type=jnp.float32)
    return (mixed_heads.astype(jnp.bfloat16), (top + jnp.log(total))[..., 0])


def attend_back(operands):
    query, keyed, valued, grad_mixed, log_total = operands
    scale = HEAD_DIM ** (-0.5)
    scores = jnp.einsum("qhd,khd->hqk", query, keyed, preferred_element_type=jnp.float32) * scale
    probs = jnp.exp(scores - log_total[..., None])
    grad_probs = jnp.einsum("qhd,khd->hqk", grad_mixed, valued, preferred_element_type=jnp.float32)
    grad_values = jnp.einsum(
        "hqk,qhd->khd", probs.astype(jnp.bfloat16), grad_mixed, preferred_element_type=jnp.float32
    )
    inner = jnp.sum(probs * grad_probs, axis=-1, keepdims=True)
    grad_scores = (probs * (grad_probs - inner)).astype(jnp.bfloat16)
    grad_query = (
        jnp.einsum("hqk,khd->qhd", grad_scores, keyed, preferred_element_type=jnp.float32) * scale
    )
    grad_keys = (
        jnp.einsum("hqk,qhd->khd", grad_scores, query, preferred_element_type=jnp.float32) * scale
    )
    return (grad_query, grad_keys, grad_values)


def per_device(
    inputs,
    cotangent,
    image_adapter_index,
    first_norm_gain,
    first_norm_bias,
    second_norm_gain,
    second_norm_bias,
    query_key_value_weight,
    attention_output_weight,
    up_weight,
    down_weight,
    up_projection_bias,
    down_projection_bias,
    query_key_value_adapter_first,
    query_key_value_adapter_second,
    projection_adapter_first,
    projection_adapter_second,
    up_adapter_first,
    up_adapter_second,
    down_adapter_first,
    down_adapter_second,
):
    head_count = lax.axis_size("heads")
    unit_count = lax.axis_size("tensor")
    fsdp_index = lax.axis_index("fsdp")
    head_index = lax.axis_index("heads")
    unit_index = lax.axis_index("tensor")
    images, length, width = inputs.shape
    adapter_factors = query_key_value_adapter_first.shape[1]
    local = jnp.arange(images, dtype=jnp.int32)
    group = fsdp_index * head_count
    own_rows = ((group + head_index) * unit_count + unit_index) * images + local
    head_rows = (
        ((group + jnp.arange(head_count, dtype=jnp.int32))[:, None] * unit_count + unit_index)
        * images
        + local[None, :]
    ).reshape(-1)
    unit_rows = (
        ((group + head_index) * unit_count + jnp.arange(unit_count, dtype=jnp.int32))[:, None]
        * images
        + local[None, :]
    ).reshape(-1)
    owned_numbers = image_adapter_index[own_rows]
    head_numbers = image_adapter_index[head_rows]
    unit_numbers = image_adapter_index[unit_rows]
    query_key_value_whole, output_whole_weight, up_rows, down_rows = (
        lax.all_gather(query_key_value_weight, "fsdp", axis=0, tiled=True),
        lax.all_gather(attention_output_weight, "fsdp", axis=0, tiled=True),
        lax.all_gather(up_weight, "fsdp", axis=0, tiled=True),
        lax.all_gather(down_weight, "fsdp", axis=0, tiled=True),
    )
    norm1, unit1, inverse1 = normalize(inputs, first_norm_gain, first_norm_bias)
    ln1_all = lax.all_gather(norm1.astype(jnp.bfloat16), "heads", axis=0, tiled=True)
    (
        query_key_value_attention,
        output_attention_part,
        query_key_value_output_weight,
        projection_input_weight,
    ) = (
        query_key_value_whole,
        output_whole_weight,
        query_key_value_adapter_second,
        projection_adapter_first,
    )
    seen = ln1_all.shape[0]
    query_key_value_input_selected = query_key_value_adapter_first[:, head_numbers]
    qkv_out_sel = query_key_value_output_weight[:, head_numbers]
    query_key_value_middle = jnp.einsum(
        "obl,holm->hobm",
        ln1_all,
        query_key_value_input_selected,
        preferred_element_type=jnp.float32,
    )
    projected = jnp.einsum(
        "isd,djf->jisf", ln1_all, query_key_value_attention, preferred_element_type=jnp.float32
    )
    projected = projected + jnp.einsum(
        "klty,klye->klte",
        query_key_value_middle,
        qkv_out_sel.astype(jnp.float32),
        precision=highest_precision,
    )
    proj_low = projected.astype(jnp.bfloat16)
    local_width = proj_low.shape[-1]
    heads_local = local_width // HEAD_DIM
    shaped = proj_low.reshape(3, seen, length, heads_local, HEAD_DIM)
    mixed_heads, log_total = lax.map(attend_forward, (shaped[0], shaped[1], shaped[2]))
    mixed_heads = mixed_heads.reshape(seen, length, local_width)
    proj_in_sel = projection_input_weight[head_numbers]
    projection_output_selected = projection_adapter_second[head_numbers]
    projection_adapter_middle = jnp.einsum(
        "lby,lyg->lbg", mixed_heads, proj_in_sel, preferred_element_type=jnp.float32
    )
    attention_branch = jnp.einsum(
        "ise,de->isd", mixed_heads, output_attention_part, preferred_element_type=jnp.float32
    )
    attention_branch = attention_branch + jnp.einsum(
        "cmt,ctf->cmf",
        projection_adapter_middle,
        projection_output_selected.astype(jnp.float32),
        precision=highest_precision,
    )
    hidden = inputs + lax.psum_scatter(
        attention_branch.astype(jnp.bfloat16), "heads", scatter_dimension=0, tiled=True
    ).astype(jnp.float32)
    norm2, unit2, inverse2 = normalize(hidden, second_norm_gain, second_norm_bias)
    second_norm_reduced = norm2.astype(jnp.bfloat16)
    up_adapter_middle = jnp.einsum(
        "ego,eoh->egh",
        second_norm_reduced,
        up_adapter_first[owned_numbers],
        preferred_element_type=jnp.float32,
    ).astype(jnp.bfloat16)
    ln2_in, up_mid_in = (
        lax.all_gather(second_norm_reduced, "tensor", axis=0, tiled=True),
        lax.all_gather(up_adapter_middle, "tensor", axis=0, tiled=True),
    )
    up_cols, down_cols, bias_cols = (up_rows, down_rows, up_projection_bias)
    up_output_columns, down_input_columns = (up_adapter_second, down_adapter_first)
    up_input_selected = up_adapter_first[unit_numbers]
    up_out_sel = up_output_columns[unit_numbers]
    down_in_sel = down_input_columns[unit_numbers]
    down_output_selected = down_adapter_second[unit_numbers]
    residual_before = jnp.einsum(
        "isd,df->isf", ln2_in, up_cols, preferred_element_type=jnp.float32
    ) + bias_cols.astype(jnp.float32)
    residual_before = residual_before + jnp.einsum(
        "cbd,cdp->cbp",
        up_mid_in.astype(jnp.float32),
        up_out_sel.astype(jnp.float32),
        precision=highest_precision,
    )
    act_low = gelu_tanh(residual_before).astype(jnp.bfloat16)
    down_adapter_middle = jnp.einsum(
        "pco,pqo->pcq", act_low, down_in_sel, preferred_element_type=jnp.float32
    )
    mlp_part = jnp.einsum("isf,df->isd", act_low, down_cols, preferred_element_type=jnp.float32)
    mlp_part = mlp_part + jnp.einsum(
        "cmt,ctf->cmf",
        down_adapter_middle,
        down_output_selected.astype(jnp.float32),
        precision=highest_precision,
    )
    mlp_sum = lax.psum_scatter(
        mlp_part.astype(jnp.bfloat16), "tensor", scatter_dimension=0, tiled=True
    ).astype(jnp.float32)
    layer_output = hidden + mlp_sum + down_projection_bias.astype(jnp.float32)
    grad_mlp = cotangent.astype(jnp.bfloat16)
    grad_mlp_in = lax.all_gather(grad_mlp, "tensor", axis=0, tiled=True)
    grad_down_mid = jnp.einsum(
        "isd,ird->isr", grad_mlp_in, down_output_selected, preferred_element_type=jnp.float32
    )
    grad_act = jnp.einsum("isd,df->isf", grad_mlp_in, down_cols, preferred_element_type=jnp.float32)
    grad_act = grad_act + jnp.einsum(
        "cbd,cdp->cbp", grad_down_mid, down_in_sel.astype(jnp.float32), precision=highest_precision
    )
    ignored, gelu_pull = jax.vjp(gelu_tanh, residual_before)
    grad_before = gelu_pull(grad_act)[0].astype(jnp.bfloat16)
    grad_up_mid = jnp.einsum(
        "pco,pqo->pcq", grad_before, up_out_sel, preferred_element_type=jnp.float32
    )
    grad_ln2 = jnp.einsum("isf,df->isd", grad_before, up_cols, preferred_element_type=jnp.float32)
    grad_ln2 = grad_ln2 + jnp.einsum(
        "isr,idr->isd",
        grad_up_mid,
        up_input_selected.astype(jnp.float32),
        precision=highest_precision,
    )
    grad_ln2 = lax.psum_scatter(
        grad_ln2.astype(jnp.bfloat16), "tensor", scatter_dimension=0, tiled=True
    ).astype(jnp.float32)
    grad_hidden = cotangent + normalize_back(grad_ln2, unit2, inverse2, second_norm_gain)
    mlp_hot = one_hot(unit_numbers, adapter_factors)
    grad_up_in_part = by_adapter(
        mlp_hot, jnp.einsum("isd,isr->idr", ln2_in, grad_up_mid, precision=highest_precision)
    )
    grad_up_out_part = by_adapter(
        mlp_hot,
        jnp.einsum("isr,isf->irf", up_mid_in, grad_before, preferred_element_type=jnp.float32),
    )
    grad_down_in_part = by_adapter(
        mlp_hot, jnp.einsum("isr,isf->irf", grad_down_mid, act_low, precision=highest_precision)
    )
    grad_down_out_part = by_adapter(
        mlp_hot,
        jnp.einsum("isr,isd->ird", down_adapter_middle, grad_mlp_in, precision=highest_precision),
    )
    grad_branch = lax.all_gather(grad_hidden.astype(jnp.bfloat16), "heads", axis=0, tiled=True)
    grad_proj_mid = jnp.einsum(
        "isd,ird->isr", grad_branch, projection_output_selected, preferred_element_type=jnp.float32
    )
    grad_mixed = jnp.einsum(
        "isd,de->ise", grad_branch, output_attention_part, preferred_element_type=jnp.float32
    )
    grad_mixed = grad_mixed + jnp.einsum(
        "isr,ier->ise", grad_proj_mid, proj_in_sel.astype(jnp.float32), precision=highest_precision
    )
    grad_mixed = grad_mixed.astype(jnp.bfloat16).reshape(seen, length, heads_local, HEAD_DIM)
    grad_query, grad_keys, grad_values = lax.map(
        attend_back, (shaped[0], shaped[1], shaped[2], grad_mixed, log_total)
    )
    grad_proj = (
        jnp.stack([grad_query, grad_keys, grad_values])
        .reshape(3, seen, length, local_width)
        .astype(jnp.bfloat16)
    )
    grad_qkv_mid = jnp.einsum(
        "jisf,jirf->jisr", grad_proj, qkv_out_sel, preferred_element_type=jnp.float32
    )
    grad_ln1 = jnp.einsum(
        "jisf,djf->isd", grad_proj, query_key_value_attention, preferred_element_type=jnp.float32
    )
    grad_ln1 = grad_ln1 + jnp.einsum(
        "jisr,jidr->isd",
        grad_qkv_mid,
        query_key_value_input_selected.astype(jnp.float32),
        precision=highest_precision,
    )
    grad_ln1 = lax.psum_scatter(
        grad_ln1.astype(jnp.bfloat16), "heads", scatter_dimension=0, tiled=True
    ).astype(jnp.float32)
    grad_input = grad_hidden + normalize_back(grad_ln1, unit1, inverse1, first_norm_gain)
    attn_hot = one_hot(head_numbers, adapter_factors)
    qkv_in_image = jnp.einsum("isd,jisr->jidr", ln1_all, grad_qkv_mid, precision=highest_precision)
    grad_qkv_in_part = jnp.einsum(
        "ia,jidr->jadr", attn_hot, qkv_in_image, precision=highest_precision
    )
    qkv_out_image = jnp.einsum(
        "jisr,jisf->jirf", query_key_value_middle, grad_proj, precision=highest_precision
    )
    grad_qkv_out_part = jnp.einsum(
        "ia,jirf->jarf", attn_hot, qkv_out_image, precision=highest_precision
    )
    grad_proj_in_part = by_adapter(
        attn_hot,
        jnp.einsum("ise,isr->ier", mixed_heads, grad_proj_mid, precision=highest_precision),
    )
    grad_proj_out_part = by_adapter(
        attn_hot,
        jnp.einsum(
            "isr,isd->ird", projection_adapter_middle, grad_branch, precision=highest_precision
        ),
    )
    grad_qkv_in, grad_proj_out, grad_up_in, grad_down_out = lax.psum(
        (grad_qkv_in_part, grad_proj_out_part, grad_up_in_part, grad_down_out_part),
        ("fsdp", "heads", "tensor"),
    )
    grad_qkv_out, grad_proj_in = lax.psum(
        (grad_qkv_out_part, grad_proj_in_part), ("fsdp", "tensor")
    )
    grad_up_out, grad_down_in = (
        lax.psum(grad_up_out_part.astype(jnp.bfloat16), ("fsdp", "heads")).astype(jnp.float32),
        lax.psum(grad_down_in_part.astype(jnp.bfloat16), ("fsdp", "heads")).astype(jnp.float32),
    )
    return (
        layer_output,
        grad_input,
        grad_qkv_in,
        grad_qkv_out,
        grad_proj_in,
        grad_proj_out,
        grad_up_in,
        grad_up_out,
        grad_down_in,
        grad_down_out,
    )


def solution(mesh):
    in_specs = (
        P(("fsdp", "heads", "tensor"), None, None),
        P(("fsdp", "heads", "tensor"), None, None),
        P(),
        P(),
        P(),
        P(),
        P(),
        P("fsdp", None, "heads"),
        P("fsdp", "heads"),
        P("fsdp", "tensor"),
        P("fsdp", "tensor"),
        P("tensor"),
        P(),
        P(),
        P(None, None, None, "heads"),
        P(None, "heads", None),
        P(),
        P(),
        P(None, None, "tensor"),
        P(None, None, "tensor"),
        P(),
    )
    out_specs = (
        P(("fsdp", "heads", "tensor"), None, None),
        P(("fsdp", "heads", "tensor"), None, None),
        P(),
        P(None, None, None, "heads"),
        P(None, "heads", None),
        P(),
        P(),
        P(None, None, "tensor"),
        P(None, None, "tensor"),
        P(),
    )
    return jax.shard_map(
        per_device, mesh=mesh, in_specs=in_specs, out_specs=out_specs, check_vma=False
    )
```

profile of v0, /device:TPU:0, one launch (start us, length us, event | category | flops | bytes accessed | tf_op | source)
XLA Modules:
  0.0 1267.5 jit_solution(7760785568148674721)
XLA Ops:
  36.3 54.6 %all-gather.13.cloned.1.call-done = bf16[1152,3,576]{2,0,1:T(8,128)(2,1)} async-done(((bf16[288,3,576]{2,0,1:T(8,128)(2,1)}), bf16[1152,3,576]{2,0,1:T(8,128)(2,1)}) %all-gather.13.cloned.1.call-update) | async-done | bytes 3981328 | tf_op jit(solution)/shard_map/all_gather | solution.py:120
  90.9 10.7 fusion.59
  109.1 57.2 %while.28 = (s32[]{:T(128)}, bf16[2,729,8,72]{1,3,2,0:T(8,128)(2,1)}, f32[2,8,729]{2,1,0:T(8,128)S(1)}, bf16[2,729,8,72]{1,3,2,0:T(8,128)(2,1)}, bf16[2,729,8,72...) while((s32[]{:T(128)}, bf16[2,729,8,72]{1,3,2,0:T(8,128)(2,1)}, ...), condition=%wide.region_5.6_spmd, body=%wide.region_2.5_spmd.sunk | while | flops 1263117824 | bytes 55831608 | solution.py:160
  109.1 9.9 multiply_reduce_fusion.8
  119.0 9.2 fusion.206
  128.2 9.3 fusion.207
  137.5 9.9 multiply_reduce_fusion.8
  156.6 9.3 fusion.207
  202.4 102.8 %all-gather.23.cloned.1.call-done = bf16[4,729,1152]{2,1,0:T(8,128)(2,1)} async-done(((bf16[1,729,1152]{2,1,0:T(8,128)(2,1)}), bf16[4,729,1152]{2,1,0:T(8,128)(2,1)}) %all-gather.23.cloned.1.call-update) | async-done | bytes 6718480 | tf_op jit(solution)/shard_map/all_gather | solution.py:222
  310.0 34.9 %all-gather.21.cloned.1.call-done = bf16[1152,1076]{1,0:T(8,128)(2,1)} async-done(((bf16[288,1076]{1,0:T(8,128)(2,1)}), bf16[1152,1076]{1,0:T(8,128)(2,1)}) %all-gather.21.cloned.1.call-update) | async-done | bytes 2479120 | tf_op jit(solution)/shard_map/all_gather | solution.py:123
  344.9 14.5 %fusion.69 = f32[4,729,1076]{1,2,0:T(8,128)} fusion(bf16[4,729,1152]{2,1,0:T(8,128)(2,1)} %all-gather.23.cloned.1.call-done, bf16[1152,1076]{1,0:T(8,128)(2,1)} %all-gather.21.cloned.1.call-done), kind=kOutput, calls=%fused_computation.114 | convolution fusion | flops 7229067264 | bytes 21748032 | tf_op jit(solution)/shard_map/isd,df->isf/dot_general | solution.py:226
  359.9 13.3 %all-gather.1 = bf16[4,729,16]{1,2,0:T(8,128)(2,1)S(1)} all-gather(bf16[1,729,16]{1,2,0:T(8,128)(2,1)S(1)} %fusion.92), channel_id=2, replica_groups=mesh['fsdp'=4,'heads'=2,'tensor'=4] {'tensor'}, dimensions={0}, use_global_device_ids=true | all-gather | bytes 116640 | tf_op jit(solution)/shard_map/all_gather | solution.py:189
  373.2 13.1 %all-gather.19.cloned.1.call-done = bf16[1152,1076]{1,0:T(8,128)(2,1)} async-done(((bf16[288,1076]{1,0:T(8,128)(2,1)}), bf16[1152,1076]{1,0:T(8,128)(2,1)}) %all-gather.19.cloned.1.call-update) | async-done | bytes 2479120 | tf_op jit(solution)/shard_map/all_gather | solution.py:122
  386.4 124.8 %all-gather.17.cloned.1.call-done = bf16[4,729,1152]{2,1,0:T(8,128)(2,1)} async-done(((bf16[1,729,1152]{2,1,0:T(8,128)(2,1)}), bf16[4,729,1152]{2,1,0:T(8,128)(2,1)}) %all-gather.17.cloned.1.call-update) | async-done | bytes 6718480 | tf_op jit(solution)/shard_map/all_gather | solution.py:188
  511.2 12.4 fusion.75
  523.6 10.1 multiply_convert_fusion.1
  533.7 18.5 %fusion.50 = bf16[4,729,1076]{1,2,0:T(8,128)(2,1)S(1)} fusion(f32[4,729,1076]{1,2,0:T(8,128)} %get-tuple-element.204, f32[4,729,1076]{1,2,0:T(8,128)} %fusion.69, f32[4,16,729]{2,1,0:T(8,128)S(1)} %fusion.138, bf16[4,16,1076]{2,1,0:T(8,128)(2,1)S(1)} %gather_fusion.7), kind=kOutput, calls=%fused_computation.72 | convolution fusion | flops 668312192 | bytes 31700512 | tf_op jit(solution)/shard_map/cbd,cdp->cbp/dot_general | solution.py:227
  555.9 13.1 %fusion.73 = f32[4,729,1152]{2,1,0:T(8,128)} fusion(bf16[4,729,1076]{1,2,0:T(8,128)(2,1)S(1)} %fusion.50, bf16[1152,1076]{1,0:T(8,128)(2,1)S(1)} %copy-done.56), kind=kOutput, calls=%fused_computation.118 | convolution fusion | flops 7229067264 | bytes 22191264 | tf_op jit(solution)/shard_map/isf,df->isd/dot_general | solution.py:235
  569.0 10.8 add_convert_fusion
  583.9 13.5 %fusion.71 = f32[4,729,1152]{2,1,0:T(8,128)S(1)} fusion(bf16[4,729,1076]{1,2,0:T(8,128)(2,1)} %get-tuple-element.203, bf16[1152,1076]{1,0:T(8,128)(2,1)S(1)} %copy-done.55), kind=kOutput, calls=%fused_computation.116 | convolution fusion | flops 7229067264 | bytes 22191264 | tf_op jit(solution)/shard_map/isf,df->isd/dot_general | solution.py:210
  606.6 90.2 %reduce-scatter.9.cloned.1.call-done = bf16[1,729,1152]{2,1,0:T(8,128)(2,1)} async-done(((bf16[4,729,1152]{2,1,0:T(8,128)(2,1)}), bf16[1,729,1152]{2,1,0:T(8,128)(2,1)}) %reduce-scatter.9.cloned.1.call-update) | async-done | bytes 1679632 | tf_op jit(solution)/shard_map/reduce_scatter | solution.py:242
  700.4 118.0 %reduce-scatter.7.cloned.1.call-done = bf16[1,729,1152]{2,1,0:T(8,128)(2,1)} async-done(((bf16[4,729,1152]{2,1,0:T(8,128)(2,1)}), bf16[1,729,1152]{2,1,0:T(8,128)(2,1)}) %reduce-scatter.7.cloned.1.call-update) | async-done | bytes 1679632 | tf_op jit(solution)/shard_map/reduce_scatter | solution.py:217
  863.4 99.9 %while.29 = (s32[]{:T(128)}, bf16[2,729,8,72]{1,3,2,0:T(8,128)(2,1)}, bf16[2,729,8,72]{1,3,2,0:T(8,128)(2,1)}, bf16[2,729,8,72]{1,3,2,0:T(8,128)(2,1)}, bf16[2,7...) while((s32[]{:T(128)}, ...), condition=%wide.region_15.16_spmd, body=%wide.region_13.15_spmd.sunk | while | flops 3112952320 | bytes 200497152 | solution.py:272
  863.9 10.1 fusion.216
  882.1 12.7 %multiply_reduce_fusion.9 = (f32[8,729]{1,0:T(8,128)S(1)}, f32[8,729,729]{1,2,0:T(8,128)}) fusion(f32[8,729,729]{1,2,0:T(8,128)} %fusion.216, f32[8,729]{1,0:T(8,128)S(1)} %dynamic-slice_bitcast_fusion.2, bf16[2,729,8,72]{1,3,2,0:T(8,128)(2,1)S(1)} %copy-done.13, s32[]{:T(128)S(6)} %copy.187, bf16[2,729,8,72]{1,3,2,0:T(8,128)(2,1)S(1)} %copy-done.9), kind=kOutput, calls=%fused_computation.30.clone.1 | convolution fusion | flops 629220288 | bytes 35830624 | tf_op jit(solution)/shard_map/while/body/eval_jaxpr/qhd,khd->hqk/dot_general | solution.py:58
  894.8 13.2 %multiply_convert_fusion.3 = bf16[8,729,729]{1,2,0:T(8,128)(2,1)S(1)} fusion(f32[8,729,729]{1,2,0:T(8,128)} %get-tuple-element.305, f32[8,729,729]{1,2,0:T(8,128)} %fusion.216, f32[8,729]{1,0:T(8,128)S(1)} %get-tuple-element.306, f32[8,729]{1,0:T(8,128)S(1)} %dynamic-slice_bitcast_fusion.2), kind=kLoop, calls=%fused_computation.29.clone.1 | loop fusion | flops 21257640 | bytes 42561936 | tf_op jit(solution)/shard_map/while/body/eval_jaxpr/convert_element_type | solution.py:63
  913.8 10.0 fusion.216
  932.0 12.6 multiply_reduce_fusion.9
  944.5 13.1 %multiply_convert_fusion.3 = bf16[8,729,729]{1,2,0:T(8,128)(2,1)S(1)} fusion(f32[8,729,729]{1,2,0:T(8,128)} %get-tuple-element.305, f32[8,729,729]{1,2,0:T(8,128)} %fusion.216, f32[8,729]{1,0:T(8,128)S(1)} %get-tuple-element.306, f32[8,729]{1,0:T(8,128)S(1)} %dynamic-slice_bitcast_fusion.2), kind=kLoop, calls=%fused_computation.29.clone.1 | loop fusion | flops 21257640 | bytes 42561936 | tf_op jit(solution)/shard_map/while/body/eval_jaxpr/convert_element_type | solution.py:63
  983.7 11.9 fusion.57
  1011.3 76.5 %all-reduce.9.cloned.1.call-done = (f32[3,8,16,576]{3,1,2,0:T(8,128)}, f32[8,576,16]{1,0,2:T(8,128)}) async-done(((f32[3,8,16,576]{3,1,2,0:T(8,128)}, f32[8,576,16]{1,0,2:T(8,128)}), (f32[3,8,16,576]{3,1,2,0:T(8,128)}, f32[8,576,16]{1,0,2:T(8,128)})) %all-reduce.9.cloned.1.call-update) | async-done | bytes 1179664 | tf_op jit(solution)/shard_map/psum | solution.py:321
  1091.8 142.8 %all-reduce.7.cloned.1.call-done = (f32[3,8,1152,16]{2,1,3,0:T(8,128)}, f32[8,16,1152]{2,0,1:T(8,128)}, f32[8,1152,16]{1,0,2:T(8,128)}, f32[8,16,1152]{2,0,1:T(8,128)}) async-done(((f32[3,8,1152,16]{2,1,3,0:T(8,128)}, f32[8,16,1152]{2,0,1:T(8,128)}, f32[8,1152,16]{1,0,2:T(8,128)}, f32[8,16,1152]{2,0,1:T(8,128)}), (f32[3,8,1152,16]{2,1,3,0:T(8,128)}, f32[8,16,1152]{2,0,1:T(8,128)}, f32[8,1152,16]{1,0,2:T(8,128)}, ...) | async-done | bytes 3538960 | tf_op jit(solution)/shard_map/psum | solution.py:317
  (288 shorter events, 242.4 us)
Async XLA Ops:
  8.0 17.2 %copy-start = (bf16[3,8,1152,16]{2,3,1,0:T(8,128)(2,1)S(1)}, bf16[3,8,1152,16]{2,3,1,0:T(8,128)(2,1)}, u32[]{:S(2)}) copy-start(bf16[3,8,1152,16]{2,3,1,0:T(8,128)(2,1)} %param.38) | copy-start | bytes 2654212
  8.0 25.2 %all-gather.11.cloned.1.call-start = ((), (), s32[]{:S(2)}) async-start(), calls=%async_computation.4 | async-start | bytes 5087232 | tf_op jit(solution)/shard_map/all_gather | solution.py:126
  17.9 73.0 %all-gather.13.cloned.1.call-start = ((), (), s32[]{:S(2)}) async-start(), calls=%async_computation.5 | async-start | bytes 5529600 | tf_op jit(solution)/shard_map/all_gather | solution.py:120
  18.6 150.3 %all-gather.15.cloned.1.call-start = ((), (), s32[]{:S(2)}) async-start(), calls=%async_computation.6 | async-start | bytes 1843200 | tf_op jit(solution)/shard_map/all_gather | solution.py:121
  19.4 170.4 %reduce-scatter.5.cloned.1.call-start = ((), (), s32[]{:S(2)}) async-start(), calls=%async_computation.7 | async-start | bytes 5087232 | tf_op jit(solution)/shard_map/reduce_scatter | solution.py:176
  25.2 76.4 %copy-start.32 = (bf16[2,3,16,576]{3,2,1,0:T(8,128)(2,1)}, bf16[2,3,16,576]{3,2,1,0:T(8,128)(2,1)S(1)}, u32[]{:S(2)}) copy-start(bf16[2,3,16,576]{3,2,1,0:T(8,128)(2,1)S(1)} %gather_fusion.2) | copy-start | bytes 331780
  25.8 75.8 %copy-start.11 = (bf16[2,3,1152,16]{2,3,1,0:T(8,128)(2,1)}, bf16[2,3,1152,16]{2,3,1,0:T(8,128)(2,1)S(1)}, u32[]{:S(2)}) copy-start(bf16[2,3,1152,16]{2,3,1,0:T(8,128)(2,1)S(1)} %gather_fusion.1) | copy-start | bytes 663556
  36.3 65.4 %copy-start.25 = (f32[3,2,729,16]{2,3,0,1:T(8,128)}, f32[3,2,729,16]{2,3,0,1:T(8,128)S(1)}, u32[]{:S(2)}) copy-start(f32[3,2,729,16]{2,3,0,1:T(8,128)S(1)} %fusion.86) | copy-start | bytes 839812
  109.1 57.2 %copy-start.21 = (bf16[2,576,16]{1,2,0:T(8,128)(2,1)S(1)}, bf16[2,576,16]{1,2,0:T(8,128)(2,1)}, u32[]{:S(2)}) copy-start(bf16[2,576,16]{1,2,0:T(8,128)(2,1)} %gather_fusion.3) | copy-start | bytes 110596
  178.4 126.8 %all-gather.23.cloned.1.call-start = ((), (), s32[]{:S(2)}) async-start(), calls=%async_computation.12 | async-start | bytes 8478720 | tf_op jit(solution)/shard_map/all_gather | solution.py:222
  181.8 163.1 %all-gather.21.cloned.1.call-start = ((), (), s32[]{:S(2)}) async-start(), calls=%async_computation.10 | async-start | bytes 3317760 | tf_op jit(solution)/shard_map/all_gather | solution.py:123
  182.4 204.0 %all-gather.19.cloned.1.call-start = ((), (), s32[]{:S(2)}) async-start(), calls=%async_computation.9 | async-start | bytes 3317760 | tf_op jit(solution)/shard_map/all_gather | solution.py:122
  182.9 328.3 %all-gather.17.cloned.1.call-start = ((), (), s32[]{:S(2)}) async-start(), calls=%async_computation.8 | async-start | bytes 8478720 | tf_op jit(solution)/shard_map/all_gather | solution.py:188
  196.7 500.0 %reduce-scatter.9.cloned.1.call-start = ((), (), s32[]{:S(2)}) async-start(), calls=%async_computation.13 | async-start | bytes 8478720 | tf_op jit(solution)/shard_map/reduce_scatter | solution.py:242
  310.0 49.4 %copy-start.14 = (bf16[1,729,1152]{2,1,0:T(8,128)(2,1)S(1)}, bf16[1,729,1152]{2,1,0:T(8,128)(2,1)}, u32[]{:S(2)}) copy-start(bf16[1,729,1152]{2,1,0:T(8,128)(2,1)} %add_convert_fusion.4) | copy-start | bytes 5038852
  373.2 150.3 %copy-start.34 = (bf16[4,729,16]{1,2,0:T(8,128)(2,1)}, bf16[4,729,16]{1,2,0:T(8,128)(2,1)S(1)}, u32[]{:S(2)}) copy-start(bf16[4,729,16]{1,2,0:T(8,128)(2,1)S(1)} %all-gather.1) | copy-start | bytes 279940
  579.8 238.6 %reduce-scatter.7.cloned.1.call-start = ((), (), s32[]{:S(2)}) async-start(), calls=%async_computation.11 | async-start | bytes 8478720 | tf_op jit(solution)/shard_map/reduce_scatter | solution.py:217
  605.9 245.4 %all-gather.25.cloned.1.call-start = ((), (), s32[]{:S(2)}) async-start(), calls=%async_computation.14 | async-start | bytes 5087232 | tf_op jit(solution)/shard_map/all_gather | solution.py:261
  696.8 121.6 %copy-start.18 = (bf16[1,729,1152]{2,1,0:T(8,128)(2,1)S(1)}, bf16[1,729,1152]{2,1,0:T(8,128)(2,1)}, u32[]{:S(2)}) copy-start(bf16[1,729,1152]{2,1,0:T(8,128)(2,1)} %reduce-scatter.9.cloned.1.call-done) | copy-start | bytes 5038852
  824.8 175.7 %all-reduce.11.cloned.1.call-start = ((), (), s32[]{:S(2)}) async-start(), calls=%async_computation.18 | async-start | bytes 1179648 | tf_op jit(solution)/shard_map/psum | solution.py:325
  833.7 13.3 %slice-start = ((s8[6782976]{0:T(1024)(128)(4,1)}), s8[2588672]{0:T(1024)(128)(4,1)S(1)}, s32[]{:S(2)}) async-start(s8[6782976]{0:T(1024)(128)(4,1)} %bitcast.261), calls=%async_computation.19 | async-start | bytes 5177344
  851.2 236.6 %all-reduce.9.cloned.1.call-start = ((), (), s32[]{:S(2)}) async-start(), calls=%async_computation.17 | async-start | bytes 2621440 | tf_op jit(solution)/shard_map/psum | solution.py:321
  863.4 99.9 %copy-start.26 = (f32[3,2,729,16]{2,3,0,1:T(8,128)S(1)}, f32[3,2,729,16]{2,3,0,1:T(8,128)}, u32[]{:S(2)}) copy-start(f32[3,2,729,16]{2,3,0,1:T(8,128)} %copy-done.25) | copy-start | bytes 839812
  894.8 13.3 %copy-start.6 = (bf16[2,729,8,72]{1,3,2,0:T(8,128)(2,1)S(1)}, bf16[2,729,8,72]{1,3,2,0:T(8,128)(2,1)}, u32[]{:S(2)}) copy-start(bf16[2,729,8,72]{1,3,2,0:T(8,128)(2,1)} %get-tuple-element.353) | copy-start | bytes 5038852 | tf_op jit(solution)/shard_map/while
  894.8 13.3 %copy-start.60 = (bf16[2,729,8,72]{1,3,2,0:T(8,128)(2,1)S(1)}, bf16[2,729,8,72]{1,3,2,0:T(8,128)(2,1)}, u32[]{:S(2)}) copy-start(bf16[2,729,8,72]{1,3,2,0:T(8,128)(2,1)} %get-tuple-element.340) | copy-start | bytes 5038852 | tf_op jit(solution)/shard_map/while
  944.5 13.1 %copy-start.6 = (bf16[2,729,8,72]{1,3,2,0:T(8,128)(2,1)S(1)}, bf16[2,729,8,72]{1,3,2,0:T(8,128)(2,1)}, u32[]{:S(2)}) copy-start(bf16[2,729,8,72]{1,3,2,0:T(8,128)(2,1)} %get-tuple-element.353) | copy-start | bytes 5038852 | tf_op jit(solution)/shard_map/while
  944.5 13.1 %copy-start.60 = (bf16[2,729,8,72]{1,3,2,0:T(8,128)(2,1)S(1)}, bf16[2,729,8,72]{1,3,2,0:T(8,128)(2,1)}, u32[]{:S(2)}) copy-start(bf16[2,729,8,72]{1,3,2,0:T(8,128)(2,1)} %get-tuple-element.340) | copy-start | bytes 5038852 | tf_op jit(solution)/shard_map/while
  972.4 262.2 %all-reduce.7.cloned.1.call-start = ((), (), s32[]{:S(2)}) async-start(), calls=%async_computation.16 | async-start | bytes 7077888 | tf_op jit(solution)/shard_map/psum | solution.py:317
  983.7 263.7 %reduce-scatter.11.cloned.1.call-start = ((), (), s32[]{:S(2)}) async-start(), calls=%async_computation.15 | async-start | bytes 5087232 | tf_op jit(solution)/shard_map/reduce_scatter | solution.py:292
  1234.6 12.7 %copy-start.40 = (f32[729]{0:T(1024)S(1)}, f32[729]{0:T(1024)}, u32[]{:S(2)}) copy-start(f32[729]{0:T(1024)} %copy-done.39) | copy-start | bytes 8752
  1234.6 12.7 %copy-start.43 = (f32[1152]{0:T(1024)S(1)}, f32[1152]{0:T(1024)}, u32[]{:S(2)}) copy-start(f32[1152]{0:T(1024)} %param.28) | copy-start | bytes 13828
  1234.7 12.7 %copy-start.48 = (f32[729]{0:T(1024)S(1)}, f32[729]{0:T(1024)}, u32[]{:S(2)}) copy-start(f32[729]{0:T(1024)} %copy-done.47) | copy-start | bytes 8752
  (60 other events, 316.2 us)
Sparse Core Ops, SparseCore 0:
  18.0 15.1 all-gather.10
  35.0 55.7 all-gather.12
  92.7 30.1 all-gather.14
  178.5 11.2 reduce-scatter.4
  824.9 12.9 all-gather.24
  851.3 55.7 all-reduce.10
  972.6 115.1 all-reduce.8
  1094.9 139.7 all-reduce.6
  1237.0 10.2 reduce-scatter.10
Sparse Core Ops, SparseCore 1:
  181.9 123.2 all-gather.22
  306.9 37.9 all-gather.20
  346.6 39.7 all-gather.18
  387.9 123.2 all-gather.16
  579.9 116.8 reduce-scatter.8
  699.2 119.1 reduce-scatter.6
where the time goes:
time: 1270 us
  waiting for transfers between devices  781 us (61%)
  matrix products  326 us (26%)
  other arithmetic  77 us (6%)
  local copies, waits for them, and re-layouts  49.9 us (4%)
  between operations  18.4 us (1%)
  blocking collectives  13.3 us (1%)
    psum x1, waiting for transfers between devices, per_device(): lax.psum((grad_qkv_in_part, grad_proj_out_part, grad_up_in_part, grad_dow...  143 us
    all_gather x1, waiting for transfers between devices, per_device(): lax.all_gather(second_norm_reduced, 'tensor', axis=0, tiled=True)  125 us
    reduce_scatter x1, waiting for transfers between devices, per_device(): lax.psum_scatter(mlp_part.astype(jnp.bfloat16), 'tensor', scatter_dimensi...  118 us
    all_gather x1, waiting for transfers between devices, per_device(): grad_mlp_in = lax.all_gather(grad_mlp, 'tensor', axis=0, tiled=True)  103 us
    reduce_scatter x1, waiting for transfers between devices, per_device(): lax.psum_scatter(grad_ln2.astype(jnp.bfloat16), 'tensor', scatter_dimensi...  90.2 us
    psum x1, waiting for transfers between devices, per_device(): lax.psum((grad_qkv_out_part, grad_proj_in_part), ('fsdp', 'tensor'))  76.5 us
    all_gather x1, waiting for transfers between devices, per_device(): lax.all_gather(query_key_value_weight, 'fsdp', axis=0, tiled=True)  54.6 us
    unnamed x129, local copies, waits for them, and re-layouts  35.5 us
  transfers between devices with their start and end apart: 15, of which 12 were waited for; matrix products, arithmetic and copies ran while one was open for 27% of the time, Pallas kernels for 0%

commit v1 on v0

--- a/solution.py
+++ b/solution.py
@@ -6,6 +6,27 @@
 HEAD_DIM = 72
 highest_precision = lax.Precision.HIGHEST
 norm_eps = 1e-06
+
+
+def collect(x, axis, dim):
+    size, index, rows = (lax.axis_size(axis), lax.axis_index(axis), x.shape[dim])
+    right = [(i, (i + 1) % size) for i in range(size)]
+    left = [(i, (i - 1) % size) for i in range(size)]
+    result = jnp.zeros((*x.shape[:dim], size * rows, *x.shape[dim + 1 :]), x.dtype)
+    result = lax.dynamic_update_slice_in_dim(result, x, index * rows, axis=dim)
+    from_left = from_right = x
+    middle = size // 2
+    for hop in range(1, middle + 1):
+        from_left = lax.ppermute(from_left, axis, right)
+        result = lax.dynamic_update_slice_in_dim(
+            result, from_left, (index - hop) % size * rows, axis=dim
+        )
+        if hop < size - middle:
+            from_right = lax.ppermute(from_right, axis, left)
+            result = lax.dynamic_update_slice_in_dim(
+                result, from_right, (index + hop) % size * rows, axis=dim
+            )
+    return result
 
 
 def normalize(values, gain, bias):
@@ -120,7 +141,7 @@
         lax.all_gather(query_key_value_weight, "fsdp", axis=0, tiled=True),
         lax.all_gather(attention_output_weight, "fsdp", axis=0, tiled=True),
         lax.all_gather(up_weight, "fsdp", axis=0, tiled=True),
-        lax.all_gather(down_weight, "fsdp", axis=0, tiled=True),
+        collect(down_weight, "fsdp", 0),
     )
     norm1, unit1, inverse1 = normalize(inputs, first_norm_gain, first_norm_bias)
     ln1_all = lax.all_gather(norm1.astype(jnp.bfloat16), "heads", axis=0, tiled=True)

time: 1270 us -> 1230 us (0.969)
  waiting for transfers between devices: 781 us -> 698 us
  local copies, waits for them, and re-layouts: 49.9 us -> 93.3 us
    all_gather x1, waiting for transfers between devices: 103 us -> 37.8 us  [per_device(): grad_mlp_in = lax.all_gather(grad_mlp, 'tensor', axis=0, tiled=True)]
    dynamic_update_slice x0 -> x4, local copies, waits for them, and re-layouts: none -> 37.4 us  [the longest x2 18.9 us: collect(): lax.dynamic_update_slice_in_dim(result, from_left, (index - hop) % size *...]
    all_gather x1 -> x0, waiting for transfers between devices: 34.9 us -> none  [per_device(): lax.all_gather(down_weight, 'fsdp', axis=0, tiled=True)]
    ppermute x0 -> x3, waiting for transfers between devices: none -> 15.7 us  [the longest x2 15.7 us: collect(): from_left = lax.ppermute(from_left, axis, right)]
    unnamed x129 -> x134, local copies, waits for them, and re-layouts: 35.5 us -> 34 us
  transfers between devices with their start and end apart: 15 -> 17, of which waited for: 12 -> 12; matrix products, arithmetic and copies ran while one was open for 27% -> 31% of each run, Pallas kernels for 0% -> 0%
where the time goes in v1:
time: 1230 us
  waiting for transfers between devices  698 us (57%)
  matrix products  321 us (26%)
  local copies, waits for them, and re-layouts  93.3 us (8%)
  other arithmetic  77 us (6%)
  between operations  18.7 us (2%)
  blocking collectives  13.4 us (1%)
    psum x1, waiting for transfers between devices, per_device(): lax.psum((grad_qkv_in_part, grad_proj_out_part, grad_up_in_part, grad_dow...  143 us
    all_gather x1, waiting for transfers between devices, per_device(): lax.all_gather(second_norm_reduced, 'tensor', axis=0, tiled=True)  125 us
    reduce_scatter x1, waiting for transfers between devices, per_device(): lax.psum_scatter(mlp_part.astype(jnp.bfloat16), 'tensor', scatter_dimensi...  118 us
    reduce_scatter x1, waiting for transfers between devices, per_device(): lax.psum_scatter(grad_ln2.astype(jnp.bfloat16), 'tensor', scatter_dimensi...  92 us
    psum x1, waiting for transfers between devices, per_device(): lax.psum((grad_qkv_out_part, grad_proj_in_part), ('fsdp', 'tensor'))  76.4 us
    all_gather x1, waiting for transfers between devices, per_device(): lax.all_gather(query_key_value_weight, 'fsdp', axis=0, tiled=True)  54.6 us
    all_gather x1, waiting for transfers between devices, per_device(): grad_mlp_in = lax.all_gather(grad_mlp, 'tensor', axis=0, tiled=True)  37.8 us
    unnamed x134, local copies, waits for them, and re-layouts  34 us
  transfers between devices with their start and end apart: 17, of which 12 were waited for; matrix products, arithmetic and copies ran while one was open for 31% of the time, Pallas kernels for 0%

profile of v1, /device:TPU:0, one launch (start us, length us, event | category | flops | bytes accessed | tf_op | source)
XLA Modules:
  0.0 1227.3 jit_solution(2007373508250236518)
XLA Ops:
  36.3 54.6 %all-gather.12.cloned.1.call-done = bf16[1152,3,576]{2,0,1:T(8,128)(2,1)} async-done(((bf16[288,3,576]{2,0,1:T(8,128)(2,1)}), bf16[1152,3,576]{2,0,1:T(8,128)(2,1)}) %all-gather.12.cloned.1.call-update) | async-done | bytes 3981328 | tf_op jit(solution)/shard_map/all_gather | solution.py:141
  90.9 10.7 fusion.59
  109.1 57.3 %while.28 = (s32[]{:T(128)}, bf16[2,729,8,72]{1,3,2,0:T(8,128)(2,1)}, f32[2,8,729]{2,1,0:T(8,128)S(1)}, bf16[2,729,8,72]{1,3,2,0:T(8,128)(2,1)}, bf16[2,729,8,72...) while((s32[]{:T(128)}, bf16[2,729,8,72]{1,3,2,0:T(8,128)(2,1)}, ...), condition=%wide.region_5.6_spmd, body=%wide.region_2.5_spmd.sunk | while | flops 1263117824 | bytes 55831608 | solution.py:181
  109.1 9.9 multiply_reduce_fusion.8
  119.1 9.2 fusion.206
  128.3 9.3 fusion.207
  137.6 9.9 multiply_reduce_fusion.8
  156.7 9.3 fusion.207
  199.9 15.7 %collective-permute-done = bf16[288,1076]{1,0:T(8,128)(2,1)S(1)} collective-permute-done((bf16[288,1076]{1,0:T(8,128)(2,1)S(1)}, bf16[288,1076]{1,0:T(8,128)(2,1)S(1)}, u32[]{:S(2)}, u32[]{:S(2)}) %collective-permute-start) | collective-permute-done | bytes 619808 | tf_op jit(solution)/shard_map/ppermute | solution.py:20
  246.4 9.8 dynamic_update_slice.32
  257.7 9.7 dynamic_update_slice.33
  267.4 37.8 %all-gather.20.cloned.1.call-done = bf16[4,729,1152]{2,1,0:T(8,128)(2,1)} async-done(((bf16[1,729,1152]{2,1,0:T(8,128)(2,1)}), bf16[4,729,1152]{2,1,0:T(8,128)(2,1)}) %all-gather.20.cloned.1.call-update) | async-done | bytes 6718480 | tf_op jit(solution)/shard_map/all_gather | solution.py:243
  319.0 13.4 %all-gather.1 = bf16[4,729,16]{1,2,0:T(8,128)(2,1)S(1)} all-gather(bf16[1,729,16]{1,2,0:T(8,128)(2,1)S(1)} %fusion.90), channel_id=2, replica_groups=mesh['fsdp'=4,'heads'=2,'tensor'=4] {'tensor'}, dimensions={0}, use_global_device_ids=true | all-gather | bytes 116640 | tf_op jit(solution)/shard_map/all_gather | solution.py:210
  332.4 12.6 %all-gather.18.cloned.1.call-done = bf16[1152,1076]{1,0:T(8,128)(2,1)} async-done(((bf16[288,1076]{1,0:T(8,128)(2,1)}), bf16[1152,1076]{1,0:T(8,128)(2,1)}) %all-gather.18.cloned.1.call-update) | async-done | bytes 2479120 | tf_op jit(solution)/shard_map/all_gather | solution.py:143
  344.9 124.7 %all-gather.16.cloned.1.call-done = bf16[4,729,1152]{2,1,0:T(8,128)(2,1)} async-done(((bf16[1,729,1152]{2,1,0:T(8,128)(2,1)}), bf16[4,729,1152]{2,1,0:T(8,128)(2,1)}) %all-gather.16.cloned.1.call-update) | async-done | bytes 6718480 | tf_op jit(solution)/shard_map/all_gather | solution.py:209
  469.6 12.4 %fusion.71 = f32[4,729,1076]{1,2,0:T(8,128)S(1)} fusion(bf16[4,729,1152]{2,1,0:T(8,128)(2,1)} %all-gather.16.cloned.1.call-done, bf16[1152,1076]{1,0:T(8,128)(2,1)} %all-gather.18.cloned.1.call-done), kind=kOutput, calls=%fused_computation.117 | convolution fusion | flops 7229067264 | bytes 21748032 | tf_op jit(solution)/shard_map/isd,df->isf/dot_general | solution.py:218
  482.0 10.0 multiply_convert_fusion.1
  492.1 22.6 %fusion.50 = bf16[4,729,1076]{1,2,0:T(8,128)(2,1)} fusion(f32[4,729,1076]{1,2,0:T(8,128)} %get-tuple-element.204, f32[4,729,1076]{1,2,0:T(8,128)} %fusion.138, bf16[4,729,1152]{2,1,0:T(8,128)(2,1)} %all-gather.20.cloned.1.call-done, bf16[1152,1076]{0,1:T(8,128)(2,1)S(1)} %copy-done.23), kind=kOutput, calls=%fused_computation.72 | convolution fusion | flops 7294955520 | bytes 40573728 | tf_op jit(solution)/shard_map/isd,df->isf/dot_general | solution.py:247
  519.4 11.8 fusion.69
  549.1 14.8 %add_convert_fusion.1 = bf16[4,729,1152]{2,1,0:T(8,128)(2,1)} fusion(f32[4,729,1152]{2,1,0:T(8,128)S(1)} %fusion.136, bf16[4,729,1076]{1,2,0:T(8,128)(2,1)} %get-tuple-element.203, bf16[1152,1076]{0,1:T(8,128)(2,1)S(1)} %copy-done.23), kind=kOutput, calls=%fused_computation.65 | convolution fusion | flops 7235785728 | bytes 28909728 | tf_op jit(solution)/shard_map/isf,df->isd/dot_general | solution.py:231
  564.5 92.0 %reduce-scatter.9.cloned.1.call-done = bf16[1,729,1152]{2,1,0:T(8,128)(2,1)} async-done(((bf16[4,729,1152]{2,1,0:T(8,128)(2,1)}), bf16[1,729,1152]{2,1,0:T(8,128)(2,1)}) %reduce-scatter.9.cloned.1.call-update) | async-done | bytes 1679632 | tf_op jit(solution)/shard_map/reduce_scatter | solution.py:263
  660.1 118.0 %reduce-scatter.7.cloned.1.call-done = bf16[1,729,1152]{2,1,0:T(8,128)(2,1)} async-done(((bf16[4,729,1152]{2,1,0:T(8,128)(2,1)}), bf16[1,729,1152]{2,1,0:T(8,128)(2,1)}) %reduce-scatter.7.cloned.1.call-update) | async-done | bytes 1679632 | tf_op jit(solution)/shard_map/reduce_scatter | solution.py:238
  823.1 100.0 %while.29 = (s32[]{:T(128)}, bf16[2,729,8,72]{1,3,2,0:T(8,128)(2,1)}, bf16[2,729,8,72]{1,3,2,0:T(8,128)(2,1)}, bf16[2,729,8,72]{1,3,2,0:T(8,128)(2,1)}, bf16[2,7...) while((s32[]{:T(128)}, ...), condition=%wide.region_15.16_spmd, body=%wide.region_13.15_spmd.sunk | while | flops 3112952320 | bytes 200497152 | solution.py:293
  823.6 10.1 fusion.216
  841.9 12.6 %multiply_reduce_fusion.9 = (f32[8,729]{1,0:T(8,128)S(1)}, f32[8,729,729]{1,2,0:T(8,128)}) fusion(f32[8,729,729]{1,2,0:T(8,128)} %fusion.216, f32[8,729]{1,0:T(8,128)S(1)} %dynamic-slice_bitcast_fusion.2, bf16[2,729,8,72]{1,3,2,0:T(8,128)(2,1)S(1)} %copy-done.13, s32[]{:T(128)S(6)} %copy.203, bf16[2,729,8,72]{1,3,2,0:T(8,128)(2,1)S(1)} %copy-done.9), kind=kOutput, calls=%fused_computation.30.clone.1 | convolution fusion | flops 629220288 | bytes 35830624 | tf_op jit(solution)/shard_map/while/body/eval_jaxpr/qhd,khd->hqk/dot_general | solution.py:79
  854.5 13.2 %multiply_convert_fusion.3 = bf16[8,729,729]{1,2,0:T(8,128)(2,1)S(1)} fusion(f32[8,729,729]{1,2,0:T(8,128)} %get-tuple-element.305, f32[8,729,729]{1,2,0:T(8,128)} %fusion.216, f32[8,729]{1,0:T(8,128)S(1)} %get-tuple-element.306, f32[8,729]{1,0:T(8,128)S(1)} %dynamic-slice_bitcast_fusion.2), kind=kLoop, calls=%fused_computation.29.clone.1 | loop fusion | flops 21257640 | bytes 42561936 | tf_op jit(solution)/shard_map/while/body/eval_jaxpr/convert_element_type | solution.py:84
  873.5 10.1 fusion.216
  891.7 12.5 %multiply_reduce_fusion.9 = (f32[8,729]{1,0:T(8,128)S(1)}, f32[8,729,729]{1,2,0:T(8,128)}) fusion(f32[8,729,729]{1,2,0:T(8,128)} %fusion.216, f32[8,729]{1,0:T(8,128)S(1)} %dynamic-slice_bitcast_fusion.2, bf16[2,729,8,72]{1,3,2,0:T(8,128)(2,1)S(1)} %copy-done.13, s32[]{:T(128)S(6)} %copy.203, bf16[2,729,8,72]{1,3,2,0:T(8,128)(2,1)S(1)} %copy-done.9), kind=kOutput, calls=%fused_computation.30.clone.1 | convolution fusion | flops 629220288 | bytes 35830624 | tf_op jit(solution)/shard_map/while/body/eval_jaxpr/qhd,khd->hqk/dot_general | solution.py:79
  904.2 13.2 %multiply_convert_fusion.3 = bf16[8,729,729]{1,2,0:T(8,128)(2,1)S(1)} fusion(f32[8,729,729]{1,2,0:T(8,128)} %get-tuple-element.305, f32[8,729,729]{1,2,0:T(8,128)} %fusion.216, f32[8,729]{1,0:T(8,128)S(1)} %get-tuple-element.306, f32[8,729]{1,0:T(8,128)S(1)} %dynamic-slice_bitcast_fusion.2), kind=kLoop, calls=%fused_computation.29.clone.1 | loop fusion | flops 21257640 | bytes 42561936 | tf_op jit(solution)/shard_map/while/body/eval_jaxpr/convert_element_type | solution.py:84
  943.5 11.9 fusion.57
  971.1 76.4 %all-reduce.9.cloned.1.call-done = (f32[3,8,16,576]{3,1,2,0:T(8,128)}, f32[8,576,16]{1,0,2:T(8,128)}) async-done(((f32[3,8,16,576]{3,1,2,0:T(8,128)}, f32[8,576,16]{1,0,2:T(8,128)}), (f32[3,8,16,576]{3,1,2,0:T(8,128)}, f32[8,576,16]{1,0,2:T(8,128)})) %all-reduce.9.cloned.1.call-update) | async-done | bytes 1179664 | tf_op jit(solution)/shard_map/psum | solution.py:342
  1051.5 142.8 %all-reduce.7.cloned.1.call-done = (f32[3,8,1152,16]{2,1,3,0:T(8,128)}, f32[8,16,1152]{2,0,1:T(8,128)}, f32[8,1152,16]{1,0,2:T(8,128)}, f32[8,16,1152]{2,0,1:T(8,128)}) async-done(((f32[3,8,1152,16]{2,1,3,0:T(8,128)}, f32[8,16,1152]{2,0,1:T(8,128)}, f32[8,1152,16]{1,0,2:T(8,128)}, f32[8,16,1152]{2,0,1:T(8,128)}), (f32[3,8,1152,16]{2,1,3,0:T(8,128)}, f32[8,16,1152]{2,0,1:T(8,128)}, f32[8,1152,16]{1,0,2:T(8,128)}, ...) | async-done | bytes 3538960 | tf_op jit(solution)/shard_map/psum | solution.py:338
  (304 shorter events, 286.8 us)
Async XLA Ops:
  8.0 17.2 %copy-start = (bf16[3,8,1152,16]{2,3,1,0:T(8,128)(2,1)S(1)}, bf16[3,8,1152,16]{2,3,1,0:T(8,128)(2,1)}, u32[]{:S(2)}) copy-start(bf16[3,8,1152,16]{2,3,1,0:T(8,128)(2,1)} %param.38) | copy-start | bytes 2654212
  8.0 25.2 %all-gather.10.cloned.1.call-start = ((), (), s32[]{:S(2)}) async-start(), calls=%async_computation.4 | async-start | bytes 5087232 | tf_op jit(solution)/shard_map/all_gather | solution.py:147
  17.9 73.0 %all-gather.12.cloned.1.call-start = ((), (), s32[]{:S(2)}) async-start(), calls=%async_computation.5 | async-start | bytes 5529600 | tf_op jit(solution)/shard_map/all_gather | solution.py:141
  18.6 150.3 %all-gather.14.cloned.1.call-start = ((), (), s32[]{:S(2)}) async-start(), calls=%async_computation.6 | async-start | bytes 1843200 | tf_op jit(solution)/shard_map/all_gather | solution.py:142
  19.4 170.4 %reduce-scatter.5.cloned.1.call-start = ((), (), s32[]{:S(2)}) async-start(), calls=%async_computation.7 | async-start | bytes 5087232 | tf_op jit(solution)/shard_map/reduce_scatter | solution.py:197
  25.2 76.4 %copy-start.38 = (bf16[2,3,16,576]{3,2,1,0:T(8,128)(2,1)}, bf16[2,3,16,576]{3,2,1,0:T(8,128)(2,1)S(1)}, u32[]{:S(2)}) copy-start(bf16[2,3,16,576]{3,2,1,0:T(8,128)(2,1)S(1)} %gather_fusion.2) | copy-start | bytes 331780
  25.8 75.8 %copy-start.11 = (bf16[2,3,1152,16]{2,3,1,0:T(8,128)(2,1)}, bf16[2,3,1152,16]{2,3,1,0:T(8,128)(2,1)S(1)}, u32[]{:S(2)}) copy-start(bf16[2,3,1152,16]{2,3,1,0:T(8,128)(2,1)S(1)} %gather_fusion.1) | copy-start | bytes 663556
  36.3 65.4 %copy-start.28 = (f32[3,2,729,16]{2,3,0,1:T(8,128)}, f32[3,2,729,16]{2,3,0,1:T(8,128)S(1)}, u32[]{:S(2)}) copy-start(f32[3,2,729,16]{2,3,0,1:T(8,128)S(1)} %fusion.84) | copy-start | bytes 839812
  109.1 57.3 %copy-start.21 = (bf16[2,576,16]{1,2,0:T(8,128)(2,1)S(1)}, bf16[2,576,16]{1,2,0:T(8,128)(2,1)}, u32[]{:S(2)}) copy-start(bf16[2,576,16]{1,2,0:T(8,128)(2,1)} %gather_fusion.3) | copy-start | bytes 110596
  178.4 126.8 %all-gather.20.cloned.1.call-start = ((), (), s32[]{:S(2)}) async-start(), calls=%async_computation.11 | async-start | bytes 8478720 | tf_op jit(solution)/shard_map/all_gather | solution.py:243
  181.9 163.1 %all-gather.18.cloned.1.call-start = ((), (), s32[]{:S(2)}) async-start(), calls=%async_computation.9 | async-start | bytes 3317760 | tf_op jit(solution)/shard_map/all_gather | solution.py:143
  182.5 287.2 %all-gather.16.cloned.1.call-start = ((), (), s32[]{:S(2)}) async-start(), calls=%async_computation.8 | async-start | bytes 8478720 | tf_op jit(solution)/shard_map/all_gather | solution.py:209
  195.0 21.9 %copy-start.3 = (s32[32]{0:T(128)S(1)}, s32[32]{0:T(128)}, u32[]{:S(2)}) copy-start(s32[32]{0:T(128)} %param.27) | copy-start | bytes 388
  195.0 24.5 %copy-start.57 = (bf16[1076]{0:T(1024)(128)(2,1)S(1)}, bf16[1076]{0:T(1024)(128)(2,1)}, u32[]{:S(2)}) copy-start(bf16[1076]{0:T(1024)(128)(2,1)} %param.36) | copy-start | bytes 6460
  195.0 24.5 %copy-start.50 = (bf16[8,16,1152]{2,1,0:T(8,128)(2,1)S(1)}, bf16[8,16,1152]{2,1,0:T(8,128)(2,1)}, u32[]{:S(2)}) copy-start(bf16[8,16,1152]{2,1,0:T(8,128)(2,1)} %param.45) | copy-start | bytes 884740
  196.8 27.0 %copy-start.20 = (bf16[8,1152,16]{1,2,0:T(8,128)(2,1)S(1)}, bf16[8,1152,16]{1,2,0:T(8,128)(2,1)}, u32[]{:S(2)}) copy-start(bf16[8,1152,16]{1,2,0:T(8,128)(2,1)} %param.42) | copy-start | bytes 884740
  196.8 459.6 %reduce-scatter.9.cloned.1.call-start = ((), (), s32[]{:S(2)}) async-start(), calls=%async_computation.12 | async-start | bytes 8478720 | tf_op jit(solution)/shard_map/reduce_scatter | solution.py:263
  196.9 18.7 %collective-permute-start = (bf16[288,1076]{1,0:T(8,128)(2,1)S(1)}, bf16[288,1076]{1,0:T(8,128)(2,1)S(1)}, u32[]{:S(2)}, u32[]{:S(2)}) collective-permute-start(bf16[288,1076]{1,0:T(8,128)(2,1)S(1)} %copy-done.30), channel_id=1, source_target_pairs={{0,8},{8,16},{16,24},{24,0},{1,9},{9,17},{17,25},{25,1},{2,10},{10... | collective-permute-start | bytes 1859336 | tf_op jit(solution)/shard_map/ppermute | solution.py:20
  198.7 46.2 %collective-permute-start.1 = (bf16[288,1076]{1,0:T(8,128)(2,1)S(1)}, bf16[288,1076]{1,0:T(8,128)(2,1)}, u32[]{:S(2)}, u32[]{:S(2)}) collective-permute-start(bf16[288,1076]{1,0:T(8,128)(2,1)S(1)} %copy-done.30), channel_id=1, source_target_pairs={{0,24},{8,0},{16,8},{24,16},{1,25},{9,1},{17,9},{25,17},{2,26},{10... | collective-permute-start | bytes 1859336 | tf_op jit(solution)/shard_map/ppermute | solution.py:25
  215.6 40.6 %collective-permute-start.2 = (bf16[288,1076]{1,0:T(8,128)(2,1)S(1)}, bf16[288,1076]{1,0:T(8,128)(2,1)}, u32[]{:S(2)}, u32[]{:S(2)}) collective-permute-start(bf16[288,1076]{1,0:T(8,128)(2,1)S(1)} %collective-permute-done), channel_id=1, source_target_pairs={{0,8},{8,16},{16,24},{24,0},{1,9},{9,17},{17,25},{25,1},{2,10},{10... | collective-permute-start | bytes 1859336 | tf_op jit(solution)/shard_map/ppermute | solution.py:20
  220.0 85.2 %copy-start.24 = (bf16[4,16,1152]{2,1,0:T(8,128)(2,1)}, bf16[4,16,1152]{2,1,0:T(8,128)(2,1)S(1)}, u32[]{:S(2)}) copy-start(bf16[4,16,1152]{2,1,0:T(8,128)(2,1)S(1)} %gather_fusion.8) | copy-start | bytes 442372
  332.4 149.6 %copy-start.40 = (bf16[4,729,16]{1,2,0:T(8,128)(2,1)}, bf16[4,729,16]{1,2,0:T(8,128)(2,1)S(1)}, u32[]{:S(2)}) copy-start(bf16[4,729,16]{1,2,0:T(8,128)(2,1)S(1)} %all-gather.1) | copy-start | bytes 279940
  332.4 149.6 %copy-start.33 = (bf16[4,16,1076]{2,1,0:T(8,128)(2,1)S(1)}, bf16[4,16,1076]{2,1,0:T(8,128)(2,1)}, u32[]{:S(2)}) copy-start(bf16[4,16,1076]{2,1,0:T(8,128)(2,1)} %gather_fusion.6) | copy-start | bytes 413188
  539.5 238.6 %reduce-scatter.7.cloned.1.call-start = ((), (), s32[]{:S(2)}) async-start(), calls=%async_computation.10 | async-start | bytes 8478720 | tf_op jit(solution)/shard_map/reduce_scatter | solution.py:238
  563.9 247.1 %all-gather.22.cloned.1.call-start = ((), (), s32[]{:S(2)}) async-start(), calls=%async_computation.13 | async-start | bytes 5087232 | tf_op jit(solution)/shard_map/all_gather | solution.py:282
  656.5 121.6 %copy-start.18 = (bf16[1,729,1152]{2,1,0:T(8,128)(2,1)S(1)}, bf16[1,729,1152]{2,1,0:T(8,128)(2,1)}, u32[]{:S(2)}) copy-start(bf16[1,729,1152]{2,1,0:T(8,128)(2,1)} %reduce-scatter.9.cloned.1.call-done) | copy-start | bytes 5038852
  784.5 175.8 %all-reduce.11.cloned.1.call-start = ((), (), s32[]{:S(2)}) async-start(), calls=%async_computation.17 | async-start | bytes 1179648 | tf_op jit(solution)/shard_map/psum | solution.py:346
  793.4 13.3 %slice-start = ((s8[6782976]{0:T(1024)(128)(4,1)}), s8[2588672]{0:T(1024)(128)(4,1)S(1)}, s32[]{:S(2)}) async-start(s8[6782976]{0:T(1024)(128)(4,1)} %bitcast.265), calls=%async_computation.18 | async-start | bytes 5177344
  810.9 236.5 %all-reduce.9.cloned.1.call-start = ((), (), s32[]{:S(2)}) async-start(), calls=%async_computation.16 | async-start | bytes 2621440 | tf_op jit(solution)/shard_map/psum | solution.py:342
  823.1 100.0 %copy-start.29 = (f32[3,2,729,16]{2,3,0,1:T(8,128)S(1)}, f32[3,2,729,16]{2,3,0,1:T(8,128)}, u32[]{:S(2)}) copy-start(f32[3,2,729,16]{2,3,0,1:T(8,128)} %copy-done.28) | copy-start | bytes 839812
  932.2 262.1 %all-reduce.7.cloned.1.call-start = ((), (), s32[]{:S(2)}) async-start(), calls=%async_computation.15 | async-start | bytes 7077888 | tf_op jit(solution)/shard_map/psum | solution.py:338
  943.4 263.6 %reduce-scatter.11.cloned.1.call-start = ((), (), s32[]{:S(2)}) async-start(), calls=%async_computation.14 | async-start | bytes 5087232 | tf_op jit(solution)/shard_map/reduce_scatter | solution.py:313
  (64 other events, 401.7 us)
Sparse Core Ops, SparseCore 0:
  18.0 15.1 all-gather.9
  35.0 55.7 all-gather.11
  92.7 30.1 all-gather.13
  178.6 11.1 reduce-scatter.4
  784.6 12.9 all-gather.21
  811.0 55.6 all-reduce.10
  932.3 115.0 all-reduce.8
  1054.5 139.7 all-reduce.6
  1196.7 10.2 reduce-scatter.10
Sparse Core Ops, SparseCore 1:
  182.0 123.2 all-gather.19
  306.9 37.9 all-gather.17
  346.4 123.2 all-gather.15
  539.6 116.8 reduce-scatter.8
  659.0 119.1 reduce-scatter.6
